TPU v7x, 128 devices: a whole 4x4x4 slice. The times are simulated.
128 devices in a mesh: gx: 16 (over y, z_lo, core), gy: 8 (over x, z_hi).
Axes of the slice: x: 4, y: 4, z: 4 (z_hi: 2, z_lo: 2; z = z_hi * 2 + z_lo), core: 2. Of those that a mesh axis runs over, the one named last changes fastest.
Arguments:
- fields: bfloat16 [8, 256, 128, 128], P(None, ('gx', 'gy')), may hold values from -6 to 6
- w_lift: bfloat16 [3, 3, 3, 8, 64], replicated, may hold values from -0.4375 to 0.4375
- b_lift: float32 [64], replicated, may hold values from -3 to 3
- down_weight: bfloat16 [4, 4, 4, 64, 64], replicated, may hold values from -0.09375 to 0.09375
- b_down: float32 [64], replicated, may hold values from -3 to 3
- perf_well: int32 [128, 256], P(('gx', 'gy')), may hold values from -1 to 2047, as said below
- perf_cell: int32 [128, 256], P(('gx', 'gy')), may hold values from 0 to 4095, as said below
- perf_weight: float32 [128, 256], P(('gx', 'gy')), may hold values from 0.25 to 2
- well_slot: int32 [2048], replicated, may hold values from 0 to 2047, each once
- well_grad: bfloat16 [2048, 64], P(('gx', 'gy')), may hold values from -24 to 24
- field_grad: bfloat16 [64, 64, 64, 128], P(None, 'gx', 'gy'), may hold values from -6 to 6
Outputs:
- coarse: bfloat16 [64, 64, 64, 128], P(None, 'gx', 'gy')
- well_feat: float32 [2048, 64], P(('gx', 'gy'))
- down_grad: float32 [4, 4, 4, 64, 64], replicated
Inputs may be any that keep to these rules, and one draw needn't show every extreme that they name: `perf_well`: entry -1 marks an empty slot. Every well appears in exactly 8 slots of one row, the perforations of one vertical well at consecutive depths. Some row has all 256 slots used in every draw. `perf_cell`: local index (x * 8 + y) * 128 + z of the perforated cell in the row's tile of 4 x 8 x 128 coarse cells; 0 in empty slots. `well_slot`: A permutation; row r is held by the device of index r // 16 along gx+gy.
All inputs are finite; a program needn't handle non-finite values.
Results may differ from a plain program's by a relative error of at most 0.0045.
Values may be sent and summed in bfloat16 or wider, within the bound.
No kernel may reach another device: no remote copies, remote signals or barrier semaphores. Data moves between devices by JAX's collectives and lax.ppermute only.
A program may use at most 128 MiB of HBM per device.

v0:
```python
import math
import jax
import jax.numpy as jnp
from jax import lax
from jax.sharding import PartitionSpec as P


def with_halo(array, sides, width):
    for axis, dim in sides:
        devices, length = (lax.axis_size(axis), array.shape[dim])
        up = [(i, (i + 1) % devices) for i in range(devices - 1)]
        down = [(j, i) for i, j in up]
        last = lax.slice_in_dim(array, length - width, length, axis=dim)
        initial = lax.slice_in_dim(array, 0, width, axis=dim)
        before = lax.ppermute(last, axis, up)
        after = lax.ppermute(initial, axis, down)
        array = jnp.concatenate([before, array, after], axis=dim)
    return array


def tile_windows(source, along_dim, pieces, tile_len, margin):
    extent = source.shape
    split_dims = extent[:along_dim] + (pieces, tile_len) + extent[along_dim + 1 :]
    leading_part = lax.slice_in_dim(source, 0, pieces * tile_len, axis=along_dim).reshape(
        split_dims
    )
    trailing = lax.slice_in_dim(source, tile_len, pieces * tile_len + 2 * margin, axis=along_dim)
    padding = [(0, 0)] * source.ndim
    padding[along_dim] = (0, tile_len - 2 * margin)
    trailing = jnp.pad(trailing, padding).reshape(split_dims)
    trailing = lax.slice_in_dim(trailing, 0, 2 * margin, axis=along_dim + 1)
    return jnp.concatenate([leading_part, trailing], axis=along_dim + 1)


def lifting(extended, w_lift, b_lift, out_width, out_height):
    full_depth = extended.shape[3]
    padded = jnp.pad(extended, ((0, 0), (0, 0), (0, 0), (1, 1)))
    channels = w_lift.shape[3]
    outputs = w_lift.shape[4]
    depth_block = min(128, full_depth)
    results = []
    for block_start in range(0, full_depth, depth_block):
        running = jnp.zeros((outputs, out_width, out_height, depth_block), jnp.float32)
        for k in range(3):
            stacked = jnp.concatenate(
                [
                    padded[
                        :,
                        i : i + out_width,
                        j : j + out_height,
                        block_start + k : block_start + k + depth_block,
                    ]
                    for i in range(3)
                    for j in range(3)
                ],
                axis=0,
            )
            kernel_taps = w_lift[:, :, k].reshape(9 * channels, outputs)
            running = running + jnp.einsum(
                "ko,kxyz->oxyz", kernel_taps, stacked, preferred_element_type=jnp.float32
            )
        active = jax.nn.gelu(running + b_lift[:, None, None, None])
        results.append(active.astype(jnp.bfloat16))
    return jnp.concatenate(results, axis=3)


def body(
    fields,
    w_lift,
    b_lift,
    down_weight,
    b_down,
    perf_well,
    perf_cell,
    perf_weight,
    well_slot,
    well_grad,
    field_grad,
):
    grid_gx = lax.axis_size("gx")
    grid_gy = lax.axis_size("gy")
    in_channels, slab_depth, grid_width, grid_height = fields.shape
    tile_width = grid_width // grid_gx
    tile_height = grid_height // grid_gy
    full_depth = slab_depth * grid_gx * grid_gy
    features = w_lift.shape[4]
    margin = 1
    padded = jnp.pad(fields, ((0, 0), (0, 0), (margin, margin), (margin, margin)))
    blocks = tile_windows(
        tile_windows(padded, 2, grid_gx, tile_width, margin), 4, grid_gy, tile_height, margin
    )
    blocks = jnp.transpose(blocks, (2, 4, 0, 1, 3, 5))
    arrived = lax.all_to_all(
        blocks.reshape((grid_gx * grid_gy,) + blocks.shape[2:]),
        ("gx", "gy"),
        split_axis=0,
        concat_axis=0,
        tiled=True,
    )
    arrived = arrived.reshape(blocks.shape)
    columns = jnp.transpose(arrived, (2, 4, 5, 0, 1, 3)).reshape(
        in_channels, tile_width + 2 * margin, tile_height + 2 * margin, full_depth
    )
    hidden = lifting(columns, w_lift, b_lift, tile_width, tile_height)
    rimmed = with_halo(hidden, (("gx", 1), ("gy", 2)), 1)
    half_width = tile_width // 2
    half_height = tile_height // 2
    half_depth = full_depth // 2
    cell_count = half_width * half_height * half_depth
    well_count = well_slot.shape[0]
    listed = perf_well[0]
    cell_ids = perf_cell[0]
    weights = perf_weight[0]
    matches = listed[:, None] == jnp.arange(well_count, dtype=jnp.int32)[None, :]
    out_slots = jnp.sum(jnp.where(matches, well_slot[None, :], 0), axis=1)
    out_slots = jnp.where(listed >= 0, out_slots, -1)
    share_fraction = lax.all_gather(well_grad, ("gx", "gy"), axis=0, tiled=True)
    chosen = out_slots[:, None] == jnp.arange(share_fraction.shape[0], dtype=jnp.int32)[None, :]
    pulled = jnp.dot(
        chosen.astype(jnp.bfloat16), share_fraction, preferred_element_type=jnp.float32
    )
    spread = pulled * weights[:, None]
    flat_grad = field_grad.astype(jnp.float32).reshape(features, cell_count)
    flat_grad = flat_grad.at[:, cell_ids].add(spread.T)
    cotangent = flat_grad.astype(jnp.bfloat16).reshape(
        features, half_width, half_height, half_depth
    )
    stretched = jnp.pad(rimmed, ((0, 0), (0, 0), (0, 0), (1, 1)))
    parity = stretched.reshape(features, half_width + 1, 2, half_height + 1, 2, half_depth + 1, 2)
    parity = jnp.transpose(parity, (2, 4, 6, 0, 1, 3, 5)).reshape(
        8 * features, half_width + 1, half_height + 1, half_depth + 1
    )
    split_weight = down_weight.reshape(2, 2, 2, 2, 2, 2, features, features)
    coarse_sum = jnp.zeros((features, half_width, half_height, half_depth), jnp.float32)
    grad_rows = []
    for a in range(2):
        grad_cols = []
        for b in range(2):
            stacked = jnp.concatenate(
                [
                    parity[:, a : a + half_width, b : b + half_height, depth : depth + half_depth]
                    for depth in range(2)
                ],
                axis=0,
            )
            kernel_taps = jnp.transpose(split_weight[a, :, b], (2, 0, 1, 3, 4, 5)).reshape(
                16 * features, features
            )
            coarse_sum = coarse_sum + jnp.einsum(
                "ko,kxyz->oxyz", kernel_taps, stacked, preferred_element_type=jnp.float32
            )
            grad_part = jnp.einsum(
                "oxyz,kxyz->ko", cotangent, stacked, preferred_element_type=jnp.float32
            )
            grad_cols.append(grad_part.reshape(2, 2, 2, 2, features, features))
        grad_rows.append(jnp.stack(grad_cols))
    local_grad = jnp.transpose(jnp.stack(grad_rows), (0, 3, 1, 4, 2, 5, 6, 7)).reshape(
        4, 4, 4, features, features
    )
    coarse = (coarse_sum + b_down[:, None, None, None]).astype(jnp.bfloat16)
    grad_scale = 1.0 / math.sqrt(cell_count * grid_gx * grid_gy)
    down_grad = lax.psum(local_grad, ("gx", "gy")) * grad_scale
    picked = (
        coarse.reshape(features, cell_count)[:, cell_ids].astype(jnp.float32) * weights[None, :]
    )
    chosen = (
        out_slots[None, :]
        == jnp.arange(well_grad.shape[0] * lax.axis_size(("gx", "gy")), dtype=jnp.int32)[:, None]
    )
    well_feat = lax.psum_scatter(
        jnp.dot(chosen.astype(jnp.float32), picked.T, precision=lax.Precision.HIGHEST),
        ("gx", "gy"),
        scatter_dimension=0,
        tiled=True,
    )
    return (coarse, well_feat, down_grad)


def solution(mesh):
    placed = (
        P(None, ("gx", "gy"), None, None),
        P(),
        P(),
        P(),
        P(),
        P(("gx", "gy"), None),
        P(("gx", "gy"), None),
        P(("gx", "gy"), None),
        P(),
        P(("gx", "gy"), None),
        P(None, "gx", "gy", None),
    )
    return jax.shard_map(
        body,
        mesh=mesh,
        in_specs=placed,
        out_specs=(P(None, "gx", "gy", None), P(("gx", "gy"), None), P()),
        check_vma=False,
    )
```

profile of v0, /device:TPU:0, one launch (start us, length us, event | category | flops | bytes accessed | tf_op | source)
XLA Modules:
  0.0 1417.5 jit_solution(12922795237270653496)
XLA Ops:
  7.2 1.6 fusion.22
  8.8 1.6 pad_slice_fusion.18
  11.7 5.0 reshape.132
  16.7 5.0 reshape.131
  21.7 6.9 maximum_bitcast_fusion
  28.6 5.7 copy.394
  34.3 9.4 reshape.192
  43.8 11.2 all-to-all-start
  56.5 14.0 all-to-all-done
  70.5 8.9 reshape.193
  79.4 5.3 copy.238
  95.2 2.3 fusion.15
  97.5 2.7 fusion.7
  101.9 1.3 collective-permute-start.1
  103.1 3.3 collective-permute-start
  106.4 334.4 %all_gather.3 = bf16[2048,64]{1,0:T(8,128)(2,1)} all-gather(bf16[16,64]{1,0:T(8,128)(2,1)S(1)} %copy-done.22), channel_id=1, replica_groups=mesh['gx'=16,'gy'=8] {'gx','gy'}, dimensions={0}, use_global_device_ids=true | all-gather | bytes 264192 | tf_op jit(solution)/shard_map/all_gather | solution.py:117
  448.3 3.1 copy.290
  451.4 1.6 fusion.21
  453.2 5.2 scatter_fusion
  458.3 2.9 convert_element_type.29
  461.3 1.3 collective-permute-start.3
  462.6 6.1 collective-permute-start.2
  468.7 3.1 collective-permute-done.3
  471.8 2.3 collective-permute-done.2
  474.1 4.5 pad_maximum_fusion.4
  478.5 11.8 copy.382
  490.3 11.5 pad.24.clone
  501.9 24.0 %reshape.136 = bf16[64,5,2,9,2,129,2]{0,6,5,4,3,2,1:T(2,128)(2,1)} reshape(bf16[64,10,18,258]{0,3,2,1:T(8,128)(2,1)} %pad.24.clone) | data formatting | bytes 11888640 | tf_op jit(solution)/shard_map/reshape | solution.py:129
  525.9 30.6 %copy.282 = bf16[2,2,2,64,5,9,129]{6,3,2,1,0,5,4:T(8,128)(2,1)} copy(bf16[2,2,2,64,5,9,129]{3,2,6,1,5,0,4:T(2,128)(2,1)} %bitcast.188) | data formatting | bytes 11888640 | tf_op jit(solution)/shard_map/transpose | solution.py:130
  556.5 27.7 %fusion.51 = (bf16[512,4,8,128]{3,0,2,1:T(8,128)(2,1)S(1)}, bf16[512,4,8,128]{3,0,2,1:T(8,128)(2,1)S(1)}, bf16[512,4,8,128]{3,0,2,1:T(8,128)(2,1)S(1)}, bf16[512...) fusion(bf16[512,5,9,129]{3,0,2,1:T(8,128)(2,1)} %bitcast.187), kind=kLoop, calls=%fused_computation.145 | loop fusion | bytes 67108864 | tf_op jit(solution)/shard_map/slice | solution.py:141
  584.2 6.7 pad_maximum_fusion.2
  591.0 2.3 fusion.61
  593.4 2.3 fusion.60
  596.8 2.0 fusion.46
  599.0 1.3 copy-done.10
  600.3 4.0 pad_maximum_fusion
  604.3 5.7 fusion.59
  610.1 2.3 fusion.58
  612.9 1.5 copy.300
  614.5 4.7 convolution_add_fusion.2
  619.1 1.4 copy-done.8
  620.5 2.0 convolution_add_fusion.1
  622.7 1.3 copy-done.5
  624.0 1.8 fusion.20
  627.2 2.0 fusion.16
  630.4 132.6 %all-reduce.7.cloned.1.call-done = f32[4,4,4,64,64]{4,3,2,1,0:T(8,128)} async-done(((f32[4,4,4,64,64]{4,3,2,1,0:T(8,128)}), f32[4,4,4,64,64]{4,3,2,1,0:T(8,128)}) %all-reduce.7.cloned.1.call-update) | async-done | bytes 1048592 | tf_op jit(solution)/shard_map/psum | solution.py:162
  762.9 3.3 broadcast_multiply_fusion
  766.2 644.2 %reduce-scatter.2.cloned.1.call-done = f32[16,64]{1,0:T(8,128)} async-done(((f32[2048,64]{1,0:T(8,128)}), f32[16,64]{1,0:T(8,128)}) %reduce-scatter.2.cloned.1.call-update) | async-done | bytes 4112 | tf_op jit(solution)/shard_map/reduce_scatter | solution.py:170
  (120 shorter events, 27.1 us)
Async XLA Ops:
  34.3 20.7 %copy-start.20 = (s32[1,256]{1,0:T(1,128)S(1)}, s32[1,256]{1,0:T(1,128)}, u32[]{:S(2)}) copy-start(s32[1,256]{1,0:T(1,128)} %param.16) | copy-start | bytes 3076
  34.3 20.7 %copy-start.21 = (s32[2048]{0:T(1024)S(1)}, s32[2048]{0:T(1024)}, u32[]{:S(2)}) copy-start(s32[2048]{0:T(1024)} %param.19) | copy-start | bytes 24580
  34.3 21.1 %copy-start.19 = (bf16[3,3,3,8,64]{4,3,2,1,0:T(8,128)(2,1)S(1)}, bf16[3,3,3,8,64]{4,3,2,1,0:T(8,128)(2,1)}, u32[]{:S(2)}) copy-start(bf16[3,3,3,8,64]{4,3,2,1,0:T(8,128)(2,1)} %param.12) | copy-start | bytes 82948
  34.3 21.1 %copy-start.15 = (bf16[4,4,4,64,64]{4,3,2,1,0:T(8,128)(2,1)S(1)}, bf16[4,4,4,64,64]{4,3,2,1,0:T(8,128)(2,1)}, u32[]{:S(2)}) copy-start(bf16[4,4,4,64,64]{4,3,2,1,0:T(8,128)(2,1)} %param.14) | copy-start | bytes 1572868
  43.8 26.7 %all-to-all-start = ((bf16[128,2,1440]{2,1,0:T(2,128)(2,1)}), bf16[128,2,1440]{2,1,0:T(2,128)(2,1)S(1)}, u32[]{:S(2)}, u32[]{:S(2)}) async-start(bf16[128,2,1440]{2,1,0:T(2,128)(2,1)} %reshape.192), calls=%async_computation | async-start | bytes 1572864 | tf_op jit(solution)/shard_map/all_to_all | solution.py:93
  54.9 708.0 %all-reduce.7.cloned.1.call-start = ((), (), s32[]{:S(2)}) async-start(), calls=%async_computation.3 | async-start | bytes 4194304 | tf_op jit(solution)/shard_map/psum | solution.py:162
  94.4 0.8 copy-start.25
  100.2 1.7 copy-start
  100.2 6.2 copy-start.22
  101.9 359.3 %collective-permute-start.1 = (bf16[64,1,16,256]{3,0,2,1:T(8,128)(2,1)}, bf16[64,1,16,256]{3,0,2,1:T(8,128)(2,1)S(1)}, u32[]{:S(2)}, u32[]{:S(2)}) collective-permute-start(bf16[64,1,16,256]{3,0,2,1:T(8,128)(2,1)} %get-tuple-element.29), channel_id=1, source_target_pairs={{8,0},{16,8},{24,16},{32,24},{40,32},{48,40},{56,48},{64,56},{72,6... | collective-permute-start | bytes 1572872 | tf_op jit(solution)/shard_map/ppermute | solution.py:16
  103.1 358.1 %collective-permute-start = (bf16[64,1,16,256]{3,0,2,1:T(8,128)(2,1)}, bf16[64,1,16,256]{3,0,2,1:T(8,128)(2,1)S(1)}, u32[]{:S(2)}, u32[]{:S(2)}) collective-permute-start(bf16[64,1,16,256]{3,0,2,1:T(8,128)(2,1)} %get-tuple-element.28), channel_id=1, source_target_pairs={{0,8},{8,16},{16,24},{24,32},{32,40},{40,48},{48,56},{56,64},{64,7... | collective-permute-start | bytes 1572872 | tf_op jit(solution)/shard_map/ppermute | solution.py:15
  446.3 6.9 copy-start.23
  458.3 2.9 copy-start.1
  461.3 10.5 collective-permute-start.3
  462.6 11.5 collective-permute-start.2
  584.2 6.7 copy-start.2
  584.2 6.7 copy-start.4
  584.2 6.7 copy-start.6
  584.2 6.7 copy-start.13
  593.3 2.4 copy-start.11
  593.4 3.5 copy-start.12
  593.4 3.5 copy-start.18
  596.8 2.2 copy-start.9
  596.8 3.5 copy-start.10
  600.3 4.0 copy-start.14
  612.9 1.5 copy-start.17
  614.4 796.1 %reduce-scatter.2.cloned.1.call-start = ((), (), s32[]{:S(2)}) async-start(), calls=%async_computation.2 | async-start | bytes 1056768 | tf_op jit(solution)/shard_map/reduce_scatter | solution.py:170
  614.4 4.7 copy-start.7
  614.5 6.1 copy-start.8
  620.5 2.2 copy-start.3
  620.5 3.5 copy-start.5
  620.5 3.5 copy-start.16
  620.5 3.5 copy-start.26
  624.0 3.2 copy-start.24
Sparse Core Ops, SparseCore 0:
  614.5 148.3 all-reduce.6
  765.9 644.5 reduce-scatter.1
where the time goes:
time: 1430 us; the launch traced here: 1420 us
  waiting for transfers between devices  796 us (56%)
  blocking collectives  334 us (23%)
  local copies, waits for them, and re-layouts  178 us (12%)
  other arithmetic  35.6 us (2%)
  matrix products  34.7 us (2%)
  starting transfers between devices  23.2 us (2%)
  between operations  15 us (1%)
    reduce_scatter x1, waiting for transfers between devices, body(): lax.psum_scatter(jnp.dot(chosen.astype(jnp.float32), picked.T, precision=...  644 us
    all_gather x1, blocking collectives, body(): share_fraction = lax.all_gather(well_grad, ('gx', 'gy'), axis=0, tiled=True)  334 us
    psum x1, waiting for transfers between devices, body(): down_grad = lax.psum(local_grad, ('gx', 'gy')) * grad_scale  133 us
    unnamed x83, local copies, waits for them, and re-layouts  48 us
    transpose x1, local copies, waits for them, and re-layouts, body(): jnp.transpose(parity, (2, 4, 6, 0, 1, 3, 5))  30.6 us
  transfers between devices with their start and end apart: 7, of which 5 were waited for; matrix products, arithmetic and copies ran while one was open for 3% of the time, Pallas kernels for 0%

commit v1 on v0

--- a/solution.py
+++ b/solution.py
@@ -114,7 +114,10 @@
     matches = listed[:, None] == jnp.arange(well_count, dtype=jnp.int32)[None, :]
     out_slots = jnp.sum(jnp.where(matches, well_slot[None, :], 0), axis=1)
     out_slots = jnp.where(listed >= 0, out_slots, -1)
-    share_fraction = lax.all_gather(well_grad, ("gx", "gy"), axis=0, tiled=True)
+    share_fraction = jnp.concatenate(
+        lax.all_to_all(jnp.stack([well_grad] * lax.axis_size(("gx", "gy"))), ("gx", "gy"), 0, 0),
+        axis=0,
+    )
     chosen = out_slots[:, None] == jnp.arange(share_fraction.shape[0], dtype=jnp.int32)[None, :]
     pulled = jnp.dot(
         chosen.astype(jnp.bfloat16), share_fraction, preferred_element_type=jnp.float32

time: 1430 us -> 1110 us (0.78)
  blocking collectives: 334 us -> 0 us
    all_gather x1 -> x0, blocking collectives: 334 us -> none  [body(): share_fraction = lax.all_gather(well_grad, ('gx', 'gy'), axis=0, tiled=True)]
    unnamed x83 -> x85, local copies, waits for them, and re-layouts: 48 us -> 53 us
  transfers between devices with their start and end apart: 7 -> 8, of which waited for: 5 -> 4; matrix products, arithmetic and copies ran while one was open for 3% -> 7% of each run, Pallas kernels for 0% -> 0%
where the time goes in v1:
time: 1110 us; the launch traced here: 1100 us
  waiting for transfers between devices  798 us (72%)
  local copies, waits for them, and re-layouts  187 us (17%)
  other arithmetic  38.5 us (3%)
  matrix products  34.7 us (3%)
  starting transfers between devices  28.6 us (3%)
  between operations  15 us (1%)
    reduce_scatter x1, waiting for transfers between devices, body(): lax.psum_scatter(jnp.dot(chosen.astype(jnp.float32), picked.T, precision=...  644 us
    psum x1, waiting for transfers between devices, body(): down_grad = lax.psum(local_grad, ('gx', 'gy')) * grad_scale  138 us
    unnamed x85, local copies, waits for them, and re-layouts  53 us
    transpose x1, local copies, waits for them, and re-layouts, body(): jnp.transpose(parity, (2, 4, 6, 0, 1, 3, 5))  30.6 us
    slice x1, local copies, waits for them, and re-layouts, body(): parity[:, a:a + half_width, b:b + half_height, depth:depth + half_depth]  27.6 us
    reshape x1, local copies, waits for them, and re-layouts, body(): stretched.reshape(features, half_width + 1, 2, half_height + 1, 2, half_d...  24 us
  transfers between devices with their start and end apart: 8, of which 4 were waited for; matrix products, arithmetic and copies ran while one was open for 7% of the time, Pallas kernels for 0%

profile of v1, /device:TPU:0, one launch (start us, length us, event | category | flops | bytes accessed | tf_op | source)
XLA Modules:
  0.0 1102.3 jit_solution(10308013215159912877)
XLA Ops:
  7.2 1.6 fusion.22
  11.7 5.0 reshape.137
  16.7 5.0 reshape.136
  21.7 6.9 maximum_bitcast_fusion
  28.6 5.7 copy.394
  34.3 9.3 reshape.198
  43.7 11.2 %all-to-all-start = ((bf16[128,2,1440]{2,1,0:T(2,128)(2,1)}), bf16[128,2,1440]{2,1,0:T(2,128)(2,1)S(1)}, u32[]{:S(2)}, u32[]{:S(2)}) async-start(bf16[128,2,1440]{2,1,0:T(2,128)(2,1)} %reshape.198), calls=%async_computation | async-start | bytes 1572864 | tf_op jit(solution)/shard_map/all_to_all | solution.py:93
  56.4 14.0 %all-to-all-done = bf16[128,2,1440]{2,1,0:T(2,128)(2,1)S(1)} async-done(((bf16[128,2,1440]{2,1,0:T(2,128)(2,1)}), bf16[128,2,1440]{2,1,0:T(2,128)(2,1)S(1)}, u32[]{:S(2)}, u32[]{:S(2)}) %all-to-all-start) | async-done | bytes 737312 | tf_op jit(solution)/shard_map/all_to_all | solution.py:93
  70.4 4.9 all-to-all-start.1
  75.4 8.9 reshape.199
  84.3 5.3 copy.238
  100.2 2.3 fusion.15
  102.4 2.7 fusion.7
  108.1 3.1 collective-permute-start
  112.2 1.9 copy.377
  114.1 1.8 reshape.182
  115.9 1.9 copy.379
  117.8 1.8 reshape.183
  119.6 1.9 copy.380
  122.6 1.9 copy.381
  124.5 1.8 reshape.185
  126.3 3.1 copy.290
  129.4 1.9 pad_maximum_fusion.10
  132.5 6.8 collective-permute-start.2
  140.5 1.6 fusion.21
  142.2 5.1 scatter_fusion
  147.4 2.9 convert_element_type.29
  150.3 2.1 collective-permute-done.2
  152.3 5.7 pad_maximum_fusion.4
  158.0 11.8 %copy.382 = bf16[64,10,18,256]{0,3,2,1:T(8,128)(2,1)} copy(bf16[64,10,18,256]{3,0,2,1:T(8,128)(2,1)} %pad_maximum_fusion.4) | data formatting | bytes 11796480
  169.8 11.5 %pad.24.clone = bf16[64,10,18,258]{0,3,2,1:T(8,128)(2,1)} pad(bf16[64,10,18,256]{0,3,2,1:T(8,128)(2,1)} %copy.382, bf16[]{:T(256)} %constant.1.clone.1), padding=0_0x0_0x0_0x1_1 | pad | bytes 11842562 | tf_op jit(solution)/shard_map/jit(_pad)/pad | solution.py:131
  181.4 24.0 %reshape.141 = bf16[64,5,2,9,2,129,2]{0,6,5,4,3,2,1:T(2,128)(2,1)} reshape(bf16[64,10,18,258]{0,3,2,1:T(8,128)(2,1)} %pad.24.clone) | data formatting | bytes 11888640 | tf_op jit(solution)/shard_map/reshape | solution.py:132
  205.4 30.6 %copy.282 = bf16[2,2,2,64,5,9,129]{6,3,2,1,0,5,4:T(8,128)(2,1)} copy(bf16[2,2,2,64,5,9,129]{3,2,6,1,5,0,4:T(2,128)(2,1)} %bitcast.189) | data formatting | bytes 11888640 | tf_op jit(solution)/shard_map/transpose | solution.py:133
  236.0 27.6 %fusion.51 = (bf16[512,4,8,128]{3,0,2,1:T(8,128)(2,1)S(1)}, bf16[512,4,8,128]{3,0,2,1:T(8,128)(2,1)S(1)}, bf16[512,4,8,128]{3,0,2,1:T(8,128)(2,1)S(1)}, bf16[512...) fusion(bf16[512,5,9,129]{3,0,2,1:T(8,128)(2,1)} %bitcast.188), kind=kLoop, calls=%fused_computation.145 | loop fusion | bytes 67108864 | tf_op jit(solution)/shard_map/slice | solution.py:144
  263.6 6.7 pad_maximum_fusion.2
  270.4 2.3 fusion.61
  272.8 2.3 fusion.60
  276.2 2.0 fusion.46
  279.7 4.0 pad_maximum_fusion
  283.7 5.7 fusion.59
  289.5 2.3 fusion.58
  293.9 4.7 convolution_add_fusion.2
  299.8 2.0 convolution_add_fusion.1
  303.2 1.8 fusion.20
  306.5 2.0 fusion.16
  309.7 138.1 %all-reduce.7.cloned.1.call-done = f32[4,4,4,64,64]{4,3,2,1,0:T(8,128)} async-done(((f32[4,4,4,64,64]{4,3,2,1,0:T(8,128)}), f32[4,4,4,64,64]{4,3,2,1,0:T(8,128)}) %all-reduce.7.cloned.1.call-update) | async-done | bytes 1048592 | tf_op jit(solution)/shard_map/psum | solution.py:165
  447.8 3.3 broadcast_multiply_fusion
  451.1 644.2 %reduce-scatter.2.cloned.1.call-done = f32[16,64]{1,0:T(8,128)} async-done(((f32[2048,64]{1,0:T(8,128)}), f32[16,64]{1,0:T(8,128)}) %reduce-scatter.2.cloned.1.call-update) | async-done | bytes 4112 | tf_op jit(solution)/shard_map/reduce_scatter | solution.py:173
  (124 shorter events, 32.2 us)
Async XLA Ops:
  34.3 20.5 %copy-start.22 = (bf16[16,64]{1,0:T(8,128)(2,1)S(1)}, bf16[16,64]{1,0:T(8,128)(2,1)}, u32[]{:S(2)}) copy-start(bf16[16,64]{1,0:T(8,128)(2,1)} %param.20) | copy-start | bytes 6148
  43.7 12.3 %copy-start.20 = (s32[1,256]{1,0:T(1,128)S(1)}, s32[1,256]{1,0:T(1,128)}, u32[]{:S(2)}) copy-start(s32[1,256]{1,0:T(1,128)} %param.16) | copy-start | bytes 3076
  43.7 12.3 %copy-start.21 = (s32[2048]{0:T(1024)S(1)}, s32[2048]{0:T(1024)}, u32[]{:S(2)}) copy-start(s32[2048]{0:T(1024)} %param.19) | copy-start | bytes 24580
  43.7 12.7 %copy-start.19 = (bf16[3,3,3,8,64]{4,3,2,1,0:T(8,128)(2,1)S(1)}, bf16[3,3,3,8,64]{4,3,2,1,0:T(8,128)(2,1)}, u32[]{:S(2)}) copy-start(bf16[3,3,3,8,64]{4,3,2,1,0:T(8,128)(2,1)} %param.12) | copy-start | bytes 82948
  43.7 26.7 %all-to-all-start = ((bf16[128,2,1440]{2,1,0:T(2,128)(2,1)}), bf16[128,2,1440]{2,1,0:T(2,128)(2,1)S(1)}, u32[]{:S(2)}, u32[]{:S(2)}) async-start(bf16[128,2,1440]{2,1,0:T(2,128)(2,1)} %reshape.198), calls=%async_computation | async-start | bytes 1572864 | tf_op jit(solution)/shard_map/all_to_all | solution.py:93
  70.4 68.9 %all-to-all-start.1 = ((bf16[128,2,512]{2,1,0:T(2,128)(2,1)}), bf16[128,2,512]{2,1,0:T(2,128)(2,1)S(1)}, u32[]{:S(2)}, u32[]{:S(2)}) async-start(bf16[128,2,512]{2,1,0:T(2,128)(2,1)} %reshape.200), calls=%async_computation.2 | async-start | bytes 524288 | tf_op jit(solution)/shard_map/all_to_all | solution.py:118
  75.3 372.5 %all-reduce.7.cloned.1.call-start = ((), (), s32[]{:S(2)}) async-start(), calls=%async_computation.4 | async-start | bytes 4194304 | tf_op jit(solution)/shard_map/psum | solution.py:165
  99.4 0.8 copy-start.25
  105.1 1.7 copy-start
  105.1 6.0 copy-start.15
  105.1 7.0 copy-start.23
  106.8 22.6 %collective-permute-start.1 = (bf16[64,1,16,256]{3,0,2,1:T(8,128)(2,1)}, bf16[64,1,16,256]{3,0,2,1:T(8,128)(2,1)S(1)}, u32[]{:S(2)}, u32[]{:S(2)}) collective-permute-start(bf16[64,1,16,256]{3,0,2,1:T(8,128)(2,1)} %get-tuple-element.29), channel_id=1, source_target_pairs={{8,0},{16,8},{24,16},{32,24},{40,32},{48,40},{56,48},{64,56},{72,6... | collective-permute-start | bytes 1572872 | tf_op jit(solution)/shard_map/ppermute | solution.py:16
  108.1 21.3 %collective-permute-start = (bf16[64,1,16,256]{3,0,2,1:T(8,128)(2,1)}, bf16[64,1,16,256]{3,0,2,1:T(8,128)(2,1)S(1)}, u32[]{:S(2)}, u32[]{:S(2)}) collective-permute-start(bf16[64,1,16,256]{3,0,2,1:T(8,128)(2,1)} %get-tuple-element.28), channel_id=1, source_target_pairs={{0,8},{8,16},{16,24},{24,32},{32,40},{40,48},{48,56},{56,64},{64,7... | collective-permute-start | bytes 1572872 | tf_op jit(solution)/shard_map/ppermute | solution.py:15
  131.3 19.0 %collective-permute-start.3 = (bf16[64,10,1,256]{3,0,2,1:T(8,128)(2,1)}, bf16[64,10,1,256]{3,0,2,1:T(8,128)(2,1)}, u32[]{:S(2)}, u32[]{:S(2)}) collective-permute-start(bf16[64,10,1,256]{3,0,2,1:T(8,128)(2,1)} %get-tuple-element.27), channel_id=1, source_target_pairs={{1,0},{2,1},{3,2},{4,3},{5,4},{6,5},{7,6},{9,8},{10,9},{11,10},{12... | collective-permute-start | bytes 983048 | tf_op jit(solution)/shard_map/ppermute | solution.py:16
  132.5 19.8 %collective-permute-start.2 = (bf16[64,10,1,256]{3,0,2,1:T(8,128)(2,1)}, bf16[64,10,1,256]{3,0,2,1:T(8,128)(2,1)}, u32[]{:S(2)}, u32[]{:S(2)}) collective-permute-start(bf16[64,10,1,256]{3,0,2,1:T(8,128)(2,1)} %get-tuple-element.26), channel_id=1, source_target_pairs={{0,1},{1,2},{2,3},{3,4},{4,5},{5,6},{6,7},{8,9},{9,10},{10,11},{11... | collective-permute-start | bytes 983048 | tf_op jit(solution)/shard_map/ppermute | solution.py:15
  147.4 5.0 copy-start.1
  263.6 6.7 copy-start.2
  263.6 6.7 copy-start.4
  263.6 6.7 copy-start.6
  263.6 6.7 copy-start.13
  272.7 2.4 copy-start.11
  272.7 3.5 copy-start.12
  272.8 3.5 copy-start.18
  276.2 2.2 copy-start.9
  276.2 3.5 copy-start.10
  279.7 4.0 copy-start.14
  292.3 1.5 copy-start.17
  293.8 801.5 %reduce-scatter.2.cloned.1.call-start = ((), (), s32[]{:S(2)}) async-start(), calls=%async_computation.3 | async-start | bytes 1056768 | tf_op jit(solution)/shard_map/reduce_scatter | solution.py:173
  293.8 4.7 copy-start.7
  293.9 5.9 copy-start.8
  299.8 2.2 copy-start.3
  299.8 3.5 copy-start.5
  299.8 3.5 copy-start.16
  299.8 3.5 copy-start.26
  303.2 3.2 copy-start.24
Sparse Core Ops, SparseCore 0:
  293.9 153.8 all-reduce.6
  450.7 644.5 reduce-scatter.1
